TPU v7x, 256 devices: a whole 4x4x8 slice. The times are simulated.
256 devices in a mesh: seq: 64 (over y, z, core), tensor: 4 (over x).
Axes of the slice: x: 4, y: 4, z: 8, core: 2. Of those that a mesh axis runs over, the one named last changes fastest.
Arguments:
- tokens: bfloat16 [32768, 3840], P('seq', 'tensor'), may hold values from -6 to 6
- w_query: bfloat16 [3840, 2048], P(None, 'tensor'), may hold values from -0.09375 to 0.09375
- w_key: bfloat16 [3840, 1024], P(None, 'tensor'), may hold values from -0.09375 to 0.09375
- w_value: bfloat16 [3840, 1024], P(None, 'tensor'), may hold values from -0.09375 to 0.09375
- query_gain: float32 [256], replicated, may hold values from 0.1 to 1.9
- key_gain: float32 [256], replicated, may hold values from 0.1 to 1.9
- adapter_down: bfloat16 [64, 64, 3840], P('seq', None, 'tensor'), may hold values from -0.09375 to 0.09375
- adapter_up: bfloat16 [64, 64, 2048], P('seq', None, 'tensor'), may hold values from -0.75 to 0.75
- adapter_ids: int32 [32768, 1], P('seq'), may hold values from 0 to 63; in each aligned block of 512 rows (0 to 511, 512 to 1023, ...) at most 16 rows name the same one
- doc_ids: int32 [32768], P('seq'), may hold values from 0 to 63, never falling along the last dimension, each value on 1 to 4096 neighbouring positions
- cotangent: bfloat16 [32768, 2048], P('seq', 'tensor'), may hold values from -6 to 6
Outputs:
- attended: bfloat16 [32768, 2048], P('seq', 'tensor')
- grad_up: float32 [64, 64, 2048], P('seq', None, 'tensor')
Inputs may be any that keep to these rules, and one draw needn't show every extreme that they name: `adapter_ids`: within the 512 tokens of one device no adapter is named by more than 16 tokens; in every draw some adapter is named by exactly 16 tokens of some device. `doc_ids`: document numbers never fall along the slab; each document has 1 to 4096 tokens and one has exactly 4096.
All inputs are finite; a program needn't handle non-finite values.
Results may differ from a plain program's by a relative error of at most 0.0088.
Values may be sent and summed in bfloat16 or wider, within the bound.
A program may use at most 128 MiB of HBM per device.

v0:
```python
import math
import jax
import jax.numpy as jnp
from jax import lax
from jax.sharding import PartitionSpec as P

HD = 256
R = 64
WINDOW = 1024
ADAPTERS = 64
CAP = 16


def passed_along(value, axis, steps):
    count = lax.axis_size(axis)
    first, last = (max(0, -steps), min(count, count - steps))
    return lax.ppermute(value, axis, [(source, source + steps) for source in range(first, last)])


def normalize(pre_field, gain_vec):
    mean_sq = jnp.mean(pre_field * pre_field, axis=-1, keepdims=True)
    return pre_field * lax.rsqrt(mean_sq + 1e-06) * gain_vec


def rotate(pre_field, positions):
    half_dim = pre_field.shape[-1] // 2
    frequency = jnp.exp(
        jnp.arange(half_dim, dtype=jnp.float32) * (-2.0 * math.log(10000.0) / pre_field.shape[-1])
    )
    angles = positions.astype(jnp.float32)[:, None] * frequency[None, :]
    cosine = jnp.cos(angles)[:, None, :]
    sine_part = jnp.sin(angles)[:, None, :]
    lower_half = pre_field[..., :half_dim]
    second = pre_field[..., half_dim:]
    return jnp.concatenate(
        [lower_half * cosine - second * sine_part, second * cosine + lower_half * sine_part],
        axis=-1,
    )


def shape_query(pre_field, gain_vec, positions):
    return rotate(normalize(pre_field, gain_vec), positions)


def attend(queries, key_rows, values, upstream, allowed):
    score_scale = 1.0 / math.sqrt(queries.shape[-1])
    scores = (
        jnp.einsum("tngd,knd->ngtk", queries, key_rows, preferred_element_type=jnp.float32)
        * score_scale
    )
    weights = jnp.where(allowed[None, None], jnp.exp(scores), 0.0)
    probs = weights / jnp.sum(weights, axis=-1, keepdims=True)
    probs_low = probs.astype(jnp.bfloat16)
    attended = jnp.einsum("ngtk,knd->tngd", probs_low, values, preferred_element_type=jnp.float32)
    dprobs = jnp.einsum("tngd,knd->ngtk", upstream, values, preferred_element_type=jnp.float32)
    delta = jnp.sum(probs * dprobs, axis=-1, keepdims=True)
    dscores = (probs * (dprobs - delta) * score_scale).astype(jnp.bfloat16)
    dqueries = jnp.einsum("ngtk,knd->tngd", dscores, key_rows, preferred_element_type=jnp.float32)
    return (attended.astype(jnp.bfloat16), dqueries)


def local(
    tokens,
    w_query,
    w_key,
    w_value,
    query_gain,
    key_gain,
    adapter_down,
    adapter_up,
    adapter_ids,
    doc_ids,
    cotangent,
):
    tok_count = tokens.shape[0]
    feat_width = tokens.shape[1]
    q_width = w_query.shape[1]
    kv_width = w_key.shape[1]
    local_heads = q_width // HD
    kv_heads = kv_width // HD
    head_group = local_heads // kv_heads
    positions = lax.axis_index("seq") * tok_count + jnp.arange(tok_count, dtype=jnp.int32)
    shard_cols = lax.all_gather(tokens, "tensor", axis=1, tiled=True)
    query_lin = jnp.dot(shard_cols, w_query, preferred_element_type=jnp.float32)
    key_lin = jnp.dot(shard_cols, w_key, preferred_element_type=jnp.float32)
    value_lin = jnp.dot(shard_cols, w_value, preferred_element_type=jnp.float32)
    token_adapter = adapter_ids[:, 0]
    chosen = token_adapter[:, None] == jnp.arange(ADAPTERS, dtype=jnp.int32)[None, :]
    before = jnp.cumsum(chosen.astype(jnp.int32), axis=0) - 1
    slot_rank = jnp.sum(jnp.where(chosen, before, 0), axis=1)
    slot_index = token_adapter * CAP + slot_rank
    dispatch = (slot_index[None, :] == jnp.arange(ADAPTERS * CAP, dtype=jnp.int32)[:, None]).astype(
        jnp.bfloat16
    )
    outgoing = jnp.dot(dispatch, tokens, preferred_element_type=jnp.float32).astype(jnp.bfloat16)
    all_down, all_up = (
        lax.all_gather(adapter_down, "seq", axis=0, tiled=True),
        lax.all_gather(adapter_up, "seq", axis=0, tiled=True),
    )
    slot_rows = outgoing.reshape(ADAPTERS, CAP, feat_width)
    partial_low = jnp.einsum(
        "acd,ard->acr", slot_rows, all_down, preferred_element_type=jnp.float32
    )
    slot_low = lax.psum(partial_low, "tensor").astype(jnp.bfloat16)
    slot_lift = jnp.einsum(
        "acr,are->ace", slot_low, all_up, preferred_element_type=jnp.float32
    ).astype(jnp.bfloat16)
    lifted = jnp.einsum(
        "st,se->te",
        dispatch,
        slot_lift.reshape(ADAPTERS * CAP, q_width),
        preferred_element_type=jnp.float32,
    ).astype(jnp.bfloat16)
    lowrank = jnp.einsum(
        "st,sr->tr",
        dispatch,
        slot_low.reshape(ADAPTERS * CAP, R),
        preferred_element_type=jnp.float32,
    ).astype(jnp.bfloat16)
    query_pre = (query_lin + lifted.astype(jnp.float32)).reshape(tok_count, local_heads, HD)
    queries, query_back = jax.vjp(
        lambda pre_query: shape_query(pre_query, query_gain, positions), query_pre
    )
    queries = queries.astype(jnp.bfloat16).reshape(tok_count, kv_heads, head_group, HD)
    key_rows = shape_query(key_lin.reshape(tok_count, kv_heads, HD), key_gain, positions).astype(
        jnp.bfloat16
    )
    values = value_lin.astype(jnp.bfloat16).reshape(tok_count, kv_heads, HD)
    rim_count = WINDOW // tok_count
    key_list = []
    value_list = []
    doc_list = []
    place_list = []
    for distance in range(rim_count, 0, -1):
        far_keys, far_values, far_docs = passed_along((key_rows, values, doc_ids), "seq", distance)
        key_list.append(far_keys)
        value_list.append(far_values)
        doc_list.append(far_docs)
        place_list.append(positions - distance * tok_count)
    key_list.append(key_rows)
    value_list.append(values)
    doc_list.append(doc_ids)
    place_list.append(positions)
    window_keys = jnp.concatenate(key_list, axis=0)
    window_values = jnp.concatenate(value_list, axis=0)
    key_docs = jnp.concatenate(doc_list, axis=0)
    key_pos = jnp.concatenate(place_list, axis=0)
    key_gap = positions[:, None] - key_pos[None, :]
    allowed = (
        (doc_ids[:, None] == key_docs[None, :])
        & (key_gap >= 0)
        & (key_gap < WINDOW)
        & (key_pos[None, :] >= 0)
    )
    upstream = cotangent.reshape(tok_count, kv_heads, head_group, HD)
    block_out, dqueries = attend(queries, window_keys, window_values, upstream, allowed)
    attended = block_out.reshape(tok_count, q_width)
    (dquery_pre,) = query_back(dqueries.reshape(tok_count, local_heads, HD))
    dquery_pre = dquery_pre.reshape(tok_count, q_width).astype(jnp.bfloat16)
    out_low = jnp.dot(dispatch, lowrank, preferred_element_type=jnp.float32).astype(jnp.bfloat16)
    out_grad = jnp.dot(dispatch, dquery_pre, preferred_element_type=jnp.float32).astype(
        jnp.bfloat16
    )
    slot_low_rows = out_low.reshape(ADAPTERS, CAP, R)
    slot_grad_rows = out_grad.reshape(ADAPTERS, CAP, q_width)
    grad_up = lax.psum_scatter(
        jnp.einsum(
            "acr,ace->are", slot_low_rows, slot_grad_rows, preferred_element_type=jnp.float32
        ),
        "seq",
        scatter_dimension=0,
        tiled=True,
    )
    return (attended, grad_up)


def solution(mesh):
    in_specs = (
        P("seq", "tensor"),
        P(None, "tensor"),
        P(None, "tensor"),
        P(None, "tensor"),
        P(),
        P(),
        P("seq", None, "tensor"),
        P("seq", None, "tensor"),
        P("seq", None),
        P("seq"),
        P("seq", "tensor"),
    )
    out_specs = (P("seq", "tensor"), P("seq", None, "tensor"))
    return jax.shard_map(local, mesh=mesh, in_specs=in_specs, out_specs=out_specs, check_vma=False)
```

profile of v0, /device:TPU:2, one launch (start us, length us, event | category | flops | bytes accessed | tf_op | source)
XLA Modules:
  0.0 409.1 jit_solution(11032409171625994337)
XLA Ops:
  9.4 1.7 collective-permute-start.3
  11.2 4.0 collective-permute-start.2
  15.9 1.2 reduce-window.6
  17.4 0.8 fusion.59
  18.9 1.0 multiply_cosine_fusion
  19.9 3.7 fusion.24
  23.7 4.0 copy.40
  27.7 2.5 fusion.16
  30.2 30.4 %all-gather.4.cloned.1.call-done = bf16[512,3840]{0,1:T(8,128)(2,1)} async-done(((bf16[512,960]{0,1:T(8,128)(2,1)}), bf16[512,3840]{0,1:T(8,128)(2,1)}) %all-gather.4.cloned.1.call-update) | async-done | bytes 3932176 | tf_op jit(solution)/shard_map/all_gather | solution.py:83
  60.7 3.5 multiply_reduce_fusion.2
  64.3 1.2 fusion.55
  66.2 2.3 collective-permute-start.5
  68.5 3.8 collective-permute-start.4
  72.3 1.9 fusion.34
  74.2 4.0 collective-permute-start.1
  78.2 2.8 collective-permute-start
  81.0 66.8 %all-gather.6.cloned.1.call-done = bf16[64,64,960]{2,1,0:T(8,128)(2,1)} async-done(((bf16[1,64,960]{2,1,0:T(8,128)(2,1)}), bf16[64,64,960]{2,1,0:T(8,128)(2,1)}) %all-gather.6.cloned.1.call-update) | async-done | bytes 7864336 | tf_op jit(solution)/shard_map/all_gather | solution.py:97
  147.8 6.3 %fusion.73 = f32[64,16,64]{2,1,0:T(8,128)S(1)} fusion(bf16[64,16,960]{2,1,0:T(8,128)(2,1)} %bitcast.128, bf16[64,64,960]{2,1,0:T(8,128)(2,1)} %all-gather.6.cloned.1.call-done), kind=kOutput, calls=%fused_computation.106 | convolution fusion | flops 125829120 | bytes 10092544 | tf_op jit(solution)/shard_map/acd,ard->acr/dot_general | solution.py:101
  154.1 20.2 %all-reduce.3 = bf16[64,16,64]{2,1,0:T(8,128)(2,1)S(1)} all-reduce(f32[64,16,64]{2,1,0:T(8,128)S(1)} %fusion.73), channel_id=1, replica_groups=mesh['seq'=64,'tensor'=4] {'tensor'}, use_global_device_ids=true, to_apply=%region_4.5 | all-reduce | flops 65536 | bytes 393216 | tf_op jit(solution)/shard_map/psum | solution.py:104
  174.4 52.3 %all-gather.8.cloned.1.call-done = bf16[64,64,512]{2,1,0:T(8,128)(2,1)} async-done(((bf16[1,64,512]{2,1,0:T(8,128)(2,1)}), bf16[64,64,512]{2,1,0:T(8,128)(2,1)}) %all-gather.8.cloned.1.call-update) | async-done | bytes 4194320 | tf_op jit(solution)/shard_map/all_gather | solution.py:98
  226.7 3.0 convolution_convert_fusion
  229.7 0.8 fusion.30
  230.5 0.8 copy-done.8
  231.2 2.3 multiply_reduce_fusion.1
  233.9 0.9 fusion.35
  235.3 3.1 fusion.5
  238.5 4.4 %fusion = (f32[2,512]{1,0:T(2,128)S(1)}, f32[1536,512,2]{1,0,2:T(8,128)S(1)}) fusion(f32[2,512]{1,0:T(2,128)S(1)} %get-tuple-element.20, f32[1536,512,2]{1,0,2:T(8,128)S(1)} %get-tuple-element.21, pred[512,1536]{0,1:T(8,128)(4,1)S(1)} %copy-done.2, bf16[64,2,8,256]{3,2,1,0:T(8,128)(2,1)S(1)} %bitcast.139, bf16[512,1,256]{2,0,1:T(8,128)(2,1)} %fusion.34, ...), kind=kOutput, calls=%fused_computation.3 | convolution fusion | flops 815528960 | bytes 14688256 | tf_op jit(solution)/shard_map/tngd,knd->ngtk/dot_general | solution.py:55
  242.9 3.8 fusion.26
  248.4 4.5 %fusion.74 = f32[64,64,512]{2,1,0:T(8,128)} fusion(bf16[64,16,64]{2,1,0:T(8,128)(2,1)S(1)} %bitcast.130, bf16[64,16,512]{2,1,0:T(8,128)(2,1)S(1)} %bitcast.129), kind=kOutput, calls=%fused_computation.107 | convolution fusion | flops 67108864 | bytes 9568256 | tf_op jit(solution)/shard_map/acr,ace->are/dot_general | solution.py:167
  253.0 5.2 %fusion.31 = bf16[256,2,512]{2,0,1:T(8,128)(2,1)S(1)} fusion(f32[2,512]{1,0:T(2,128)S(1)} %get-tuple-element.20, f32[1536,512,2]{1,0,2:T(8,128)} %copy-done.11, pred[512,1536]{0,1:T(8,128)(4,1)S(1)} %copy-done.2, bf16[512,1,256]{2,0,1:T(8,128)(2,1)} %fusion.34, bf16[512,1,256]{2,0,1:T(8,128)(2,1)} %collective-permute-done.1, ...), kind=kOutput, calls=%fused_computation.35 | convolution fusion | flops 814219264 | bytes 8392704 | tf_op jit(solution)/shard_map/ngtk,knd->tngd/dot_general | solution.py:54
  258.2 1.0 copy.52
  259.2 143.4 %reduce-scatter.2.cloned.1.call-done = f32[1,64,512]{2,1,0:T(8,128)} async-done(((f32[64,64,512]{2,1,0:T(8,128)}), f32[1,64,512]{2,1,0:T(8,128)}) %reduce-scatter.2.cloned.1.call-update) | async-done | bytes 131088 | tf_op jit(solution)/shard_map/reduce_scatter | solution.py:166
  (63 shorter events, 7.4 us)
Async XLA Ops:
  7.2 53.5 %copy-start = (bf16[3840,256]{1,0:T(8,128)(2,1)S(1)}, bf16[3840,256]{1,0:T(8,128)(2,1)}, u32[]{:S(2)}) copy-start(bf16[3840,256]{1,0:T(8,128)(2,1)} %param.13) | copy-start | bytes 5898244
  7.2 53.5 %all-gather.4.cloned.1.call-start = ((), (), s32[]{:S(2)}) async-start(), calls=%async_computation.1 | async-start | bytes 4915200 | tf_op jit(solution)/shard_map/all_gather | solution.py:83
  7.9 139.9 %all-gather.6.cloned.1.call-start = ((), (), s32[]{:S(2)}) async-start(), calls=%async_computation.2 | async-start | bytes 8519680 | tf_op jit(solution)/shard_map/all_gather | solution.py:97
  8.7 218.0 %all-gather.8.cloned.1.call-start = ((), (), s32[]{:S(2)}) async-start(), calls=%async_computation.3 | async-start | bytes 4259840 | tf_op jit(solution)/shard_map/all_gather | solution.py:98
  9.4 393.2 %reduce-scatter.2.cloned.1.call-start = ((), (), s32[]{:S(2)}) async-start(), calls=%async_computation.4 | async-start | bytes 8519680 | tf_op jit(solution)/shard_map/reduce_scatter | solution.py:166
  9.4 18.2 %collective-permute-start.3 = (s32[512]{0:T(512)}, s32[512]{0:T(512)S(1)}, u32[]{:S(2)}, u32[]{:S(2)}) collective-permute-start(s32[512]{0:T(512)} %param.20), channel_id=1, source_target_pairs={{0,4},{4,8},{8,12},{12,16},{16,20},{20,24},{24,28},{28,32},{32,36}... | collective-permute-start | bytes 6152 | tf_op jit(solution)/shard_map/ppermute | solution.py:17
  11.2 16.5 %collective-permute-start.2 = (s32[512]{0:T(512)}, s32[512]{0:T(512)S(1)}, u32[]{:S(2)}, u32[]{:S(2)}) collective-permute-start(s32[512]{0:T(512)} %param.20), channel_id=1, source_target_pairs={{0,8},{4,12},{8,16},{12,20},{16,24},{20,28},{24,32},{28,36},{32,40... | collective-permute-start | bytes 6152 | tf_op jit(solution)/shard_map/ppermute | solution.py:17
  23.7 4.0 copy-start.4
  30.2 34.0 %copy-start.5 = (f32[256]{0:T(256)S(1)}, f32[256]{0:T(256)}, u32[]{:S(2)}) copy-start(f32[256]{0:T(256)} %param.16) | copy-start | bytes 3076
  60.7 11.6 %copy-start.7 = (bf16[512,3840]{0,1:T(8,128)(2,1)S(1)}, bf16[512,3840]{0,1:T(8,128)(2,1)}, u32[]{:S(2)}) copy-start(bf16[512,3840]{0,1:T(8,128)(2,1)} %all-gather.4.cloned.1.call-done) | copy-start | bytes 11796484
  60.7 11.6 %copy-start.9 = (bf16[3840,256]{1,0:T(8,128)(2,1)S(1)}, bf16[3840,256]{1,0:T(8,128)(2,1)}, u32[]{:S(2)}) copy-start(bf16[3840,256]{1,0:T(8,128)(2,1)} %param.14) | copy-start | bytes 5898244
  66.2 169.1 %collective-permute-start.5 = (bf16[512,1,256]{0,2,1:T(8,128)(2,1)}, bf16[512,1,256]{0,2,1:T(8,128)(2,1)}, u32[]{:S(2)}, u32[]{:S(2)}) collective-permute-start(bf16[512,1,256]{0,2,1:T(8,128)(2,1)} %pad_maximum_fusion), channel_id=1, source_target_pairs={{0,4},{4,8},{8,12},{12,16},{16,20},{20,24},{24,28},{28,32},{32,36}... | collective-permute-start | bytes 786440 | tf_op jit(solution)/shard_map/ppermute | solution.py:17
  68.5 166.8 %collective-permute-start.4 = (bf16[512,1,256]{0,2,1:T(8,128)(2,1)}, bf16[512,1,256]{0,2,1:T(8,128)(2,1)}, u32[]{:S(2)}, u32[]{:S(2)}) collective-permute-start(bf16[512,1,256]{0,2,1:T(8,128)(2,1)} %pad_maximum_fusion), channel_id=1, source_target_pairs={{0,8},{4,12},{8,16},{12,20},{16,24},{20,28},{24,32},{28,36},{32,40... | collective-permute-start | bytes 786440 | tf_op jit(solution)/shard_map/ppermute | solution.py:17
  74.2 164.2 %collective-permute-start.1 = (bf16[512,1,256]{2,0,1:T(8,128)(2,1)}, bf16[512,1,256]{2,0,1:T(8,128)(2,1)}, u32[]{:S(2)}, u32[]{:S(2)}) collective-permute-start(bf16[512,1,256]{2,0,1:T(8,128)(2,1)} %fusion.34), channel_id=1, source_target_pairs={{0,4},{4,8},{8,12},{12,16},{16,20},{20,24},{24,28},{28,32},{32,36}... | collective-permute-start | bytes 786440 | tf_op jit(solution)/shard_map/ppermute | solution.py:17
  78.2 160.2 %collective-permute-start = (bf16[512,1,256]{2,0,1:T(8,128)(2,1)}, bf16[512,1,256]{2,0,1:T(8,128)(2,1)}, u32[]{:S(2)}, u32[]{:S(2)}) collective-permute-start(bf16[512,1,256]{2,0,1:T(8,128)(2,1)} %fusion.34), channel_id=1, source_target_pairs={{0,8},{4,12},{8,16},{12,20},{16,24},{20,28},{24,32},{28,36},{32,40... | collective-permute-start | bytes 786440 | tf_op jit(solution)/shard_map/ppermute | solution.py:17
  226.7 3.8 copy-start.6
  226.7 4.6 %copy-start.8 = (bf16[512,3840]{0,1:T(8,128)(2,1)S(1)}, bf16[512,3840]{0,1:T(8,128)(2,1)}, u32[]{:S(2)}) copy-start(bf16[512,3840]{0,1:T(8,128)(2,1)} %all-gather.4.cloned.1.call-done) | copy-start | bytes 11796484
  233.5 1.4 copy-start.3
  233.8 1.5 copy-start.2
  235.3 3.1 copy-start.10
  238.4 4.5 %copy-start.11 = (f32[1536,512,2]{1,0,2:T(8,128)}, f32[1536,512,2]{1,0,2:T(8,128)S(1)}, u32[]{:S(2)}) copy-start(f32[1536,512,2]{1,0,2:T(8,128)S(1)} %get-tuple-element.21) | copy-start | bytes 18874372
  253.0 149.6 %copy-start.1 = (bf16[3840,256]{1,0:T(8,128)(2,1)S(1)}, bf16[3840,256]{1,0:T(8,128)(2,1)}, u32[]{:S(2)}) copy-start(bf16[3840,256]{1,0:T(8,128)(2,1)} %param.13) | copy-start | bytes 5898244
Sparse Core Ops, SparseCore 0:
  9.8 50.8 all-gather.3
  63.4 84.3 all-gather.5
  150.6 76.0 all-gather.7
  253.1 149.4 reduce-scatter.1
where the time goes:
time: 410 us; the launch traced here: 409 us
  waiting for transfers between devices  295 us (72%)
  matrix products  44.1 us (11%)
  blocking collectives  20.2 us (5%)
  starting transfers between devices  18.7 us (5%)
  between operations  14.1 us (3%)
  other arithmetic  10.1 us (2%)
  local copies, waits for them, and re-layouts  6.79 us (2%)
    reduce_scatter x1, waiting for transfers between devices, local(): lax.psum_scatter(jnp.einsum('acr,ace->are', slot_low_rows, slot_grad_rows...  143 us
    all_gather x1, waiting for transfers between devices, local(): lax.all_gather(adapter_down, 'seq', axis=0, tiled=True)  66.8 us
    all_gather x1, waiting for transfers between devices, local(): lax.all_gather(adapter_up, 'seq', axis=0, tiled=True)  52.3 us
    all_gather x1, waiting for transfers between devices, local(): shard_cols = lax.all_gather(tokens, 'tensor', axis=1, tiled=True)  30.4 us
    psum x1, blocking collectives, local(): slot_low = lax.psum(partial_low, 'tensor').astype(jnp.bfloat16)  20.2 us
    ppermute x6, starting transfers between devices, passed_along(): lax.ppermute(value, axis, [(source, source + steps) for source in range(f...  18.6 us
  transfers between devices with their start and end apart: 10, of which 4 were waited for; matrix products, arithmetic and copies ran while one was open for 11% of the time, Pallas kernels for 0%

commit v1 on v0

--- a/solution.py
+++ b/solution.py
@@ -3,6 +3,7 @@
 import jax.numpy as jnp
 from jax import lax
 from jax.sharding import PartitionSpec as P
+from jax.lax import all_to_all, psum
 
 HD = 256
 R = 64
@@ -80,7 +81,9 @@
     kv_heads = kv_width // HD
     head_group = local_heads // kv_heads
     positions = lax.axis_index("seq") * tok_count + jnp.arange(tok_count, dtype=jnp.int32)
-    shard_cols = lax.all_gather(tokens, "tensor", axis=1, tiled=True)
+    all_values = jnp.stack([tokens for _ in range(psum(1, "tensor"))])
+    kept_arr = all_to_all(all_values, "tensor", 0, 0)
+    shard_cols = jnp.concatenate(kept_arr, axis=1)
     query_lin = jnp.dot(shard_cols, w_query, preferred_element_type=jnp.float32)
     key_lin = jnp.dot(shard_cols, w_key, preferred_element_type=jnp.float32)
     value_lin = jnp.dot(shard_cols, w_value, preferred_element_type=jnp.float32)

time: 410 us -> 368 us (0.90)
  waiting for transfers between devices: 295 us -> 243 us
  starting transfers between devices: 18.7 us -> 25 us
    all_gather x1, waiting for transfers between devices: 66.8 us -> 19.3 us  [local(): lax.all_gather(adapter_down, 'seq', axis=0, tiled=True)]
    all_gather x1 -> x0, waiting for transfers between devices: 30.4 us -> none  [local(): shard_cols = lax.all_gather(tokens, 'tensor', axis=1, tiled=True)]
    all_to_all x0 -> x1, waiting for transfers between devices: none -> 27.3 us  [local(): kept_arr = all_to_all(all_values, 'tensor', 0, 0)]
    all_to_all x0 -> x1, starting transfers between devices: none -> 7.18 us  [local(): kept_arr = all_to_all(all_values, 'tensor', 0, 0)]
  transfers between devices with their start and end apart: 10 -> 10, of which waited for: 4 -> 4; matrix products, arithmetic and copies ran while one was open for 11% -> 14% of each run, Pallas kernels for 0% -> 0%
where the time goes in v1:
time: 368 us
  waiting for transfers between devices  243 us (66%)
  matrix products  47.7 us (13%)
  starting transfers between devices  25 us (7%)
  blocking collectives  20.3 us (6%)
  between operations  14.1 us (4%)
  local copies, waits for them, and re-layouts  9.31 us (3%)
  other arithmetic  8.05 us (2%)
    reduce_scatter x1, waiting for transfers between devices, local(): lax.psum_scatter(jnp.einsum('acr,ace->are', slot_low_rows, slot_grad_rows...  143 us
    all_gather x1, waiting for transfers between devices, local(): lax.all_gather(adapter_up, 'seq', axis=0, tiled=True)  52.1 us
    all_to_all x1, waiting for transfers between devices, local(): kept_arr = all_to_all(all_values, 'tensor', 0, 0)  27.3 us
    psum x1, blocking collectives, local(): slot_low = lax.psum(partial_low, 'tensor').astype(jnp.bfloat16)  20.3 us
    all_gather x1, waiting for transfers between devices, local(): lax.all_gather(adapter_down, 'seq', axis=0, tiled=True)  19.3 us
    ppermute x6, starting transfers between devices, passed_along(): lax.ppermute(value, axis, [(source, source + steps) for source in range(f...  17.7 us
  transfers between devices with their start and end apart: 10, of which 4 were waited for; matrix products, arithmetic and copies ran while one was open for 14% of the time, Pallas kernels for 0%

profile of v1, /device:TPU:2, one launch (start us, length us, event | category | flops | bytes accessed | tf_op | source)
XLA Modules:
  0.0 367.9 jit_solution(12470993814805625501)
XLA Ops:
  8.7 3.4 stack.2
  12.1 7.2 %all-to-all-start = ((bf16[4,512,960]{1,2,0:T(8,128)(2,1)}), bf16[4,512,960]{1,2,0:T(8,128)(2,1)}, u32[]{:S(2)}, u32[]{:S(2)}) async-start(bf16[4,512,960]{1,2,0:T(8,128)(2,1)} %stack.2), calls=%async_computation | async-start | bytes 7864320 | tf_op jit(solution)/shard_map/all_to_all | solution.py:85
  19.2 1.3 collective-permute-start.3
  20.5 2.7 collective-permute-start.2
  23.3 1.2 reduce-window.6
  25.0 1.0 multiply_cosine_fusion
  26.0 2.5 fusion.24
  28.5 3.9 %copy.41 = bf16[1024,960]{1,0:T(8,128)(2,1)} copy(bf16[1024,960]{0,1:T(8,128)(2,1)} %fusion.24) | data formatting | bytes 3932160 | tf_op jit(solution)/shard_map/convert_element_type | solution.py:98
  32.4 2.5 fusion.16
  35.0 27.3 %all-to-all-done = bf16[4,512,960]{1,2,0:T(8,128)(2,1)} async-done(((bf16[4,512,960]{1,2,0:T(8,128)(2,1)}), bf16[4,512,960]{1,2,0:T(8,128)(2,1)}, u32[]{:S(2)}, u32[]{:S(2)}) %all-to-all-start) | async-done | bytes 3932192 | tf_op jit(solution)/shard_map/all_to_all | solution.py:85
  62.2 4.0 %multiply_reduce_fusion.2 = (f32[512]{0:T(512)S(1)}, f32[512,256]{0,1:T(8,128)S(1)}) fusion(bf16[512,3840]{0,1:T(8,128)(2,1)} %bitcast.1, bf16[3840,256]{1,0:T(8,128)(2,1)S(1)} %copy-done), kind=kOutput, calls=%fused_computation.63 | convolution fusion | flops 1006894592 | bytes 6424576 | tf_op jit(solution)/shard_map/dot_general | solution.py:88
  66.4 1.2 fusion.55
  68.3 2.0 collective-permute-start.5
  70.3 4.4 %collective-permute-start.4 = (bf16[512,1,256]{0,2,1:T(8,128)(2,1)}, bf16[512,1,256]{0,2,1:T(8,128)(2,1)}, u32[]{:S(2)}, u32[]{:S(2)}) collective-permute-start(bf16[512,1,256]{0,2,1:T(8,128)(2,1)} %pad_maximum_fusion), channel_id=1, source_target_pairs={{0,8},{4,12},{8,16},{12,20},{16,24},{20,28},{24,32},{28,36},{32,40... | collective-permute-start | bytes 786440 | tf_op jit(solution)/shard_map/ppermute | solution.py:18
  74.6 4.1 %fusion.34 = bf16[512,1,256]{2,0,1:T(8,128)(2,1)} fusion(bf16[512,3840]{0,1:T(8,128)(2,1)} %bitcast.1, bf16[3840,256]{1,0:T(8,128)(2,1)S(1)} %copy-done.9), kind=kOutput, calls=%fused_computation.37 | convolution fusion | flops 1006764032 | bytes 6160384 | tf_op jit(solution)/shard_map/dot_general | solution.py:89
  78.7 4.1 %collective-permute-start.1 = (bf16[512,1,256]{2,0,1:T(8,128)(2,1)}, bf16[512,1,256]{2,0,1:T(8,128)(2,1)}, u32[]{:S(2)}, u32[]{:S(2)}) collective-permute-start(bf16[512,1,256]{2,0,1:T(8,128)(2,1)} %fusion.34), channel_id=1, source_target_pairs={{0,4},{4,8},{8,12},{12,16},{16,20},{20,24},{24,28},{28,32},{32,36}... | collective-permute-start | bytes 786440 | tf_op jit(solution)/shard_map/ppermute | solution.py:18
  82.8 3.3 collective-permute-start
  86.1 19.3 %all-gather.3.cloned.1.call-done = bf16[64,64,960]{2,1,0:T(8,128)(2,1)} async-done(((bf16[1,64,960]{2,1,0:T(8,128)(2,1)}), bf16[64,64,960]{2,1,0:T(8,128)(2,1)}) %all-gather.3.cloned.1.call-update) | async-done | bytes 7864336 | tf_op jit(solution)/shard_map/all_gather | solution.py:100
  105.5 6.3 %fusion.73 = f32[64,16,64]{2,1,0:T(8,128)S(1)} fusion(bf16[64,16,960]{2,1,0:T(8,128)(2,1)} %bitcast.131, bf16[64,64,960]{2,1,0:T(8,128)(2,1)} %all-gather.3.cloned.1.call-done), kind=kOutput, calls=%fused_computation.106 | convolution fusion | flops 125829120 | bytes 10092544 | tf_op jit(solution)/shard_map/acd,ard->acr/dot_general | solution.py:104
  111.7 20.3 %all-reduce.3 = bf16[64,16,64]{2,1,0:T(8,128)(2,1)S(1)} all-reduce(f32[64,16,64]{2,1,0:T(8,128)S(1)} %fusion.73), channel_id=1, replica_groups=mesh['seq'=64,'tensor'=4] {'tensor'}, use_global_device_ids=true, to_apply=%region_4.5 | all-reduce | flops 65536 | bytes 393216 | tf_op jit(solution)/shard_map/psum | solution.py:107
  132.1 52.1 %all-gather.5.cloned.1.call-done = bf16[64,64,512]{2,1,0:T(8,128)(2,1)} async-done(((bf16[1,64,512]{2,1,0:T(8,128)(2,1)}), bf16[64,64,512]{2,1,0:T(8,128)(2,1)}) %all-gather.5.cloned.1.call-update) | async-done | bytes 4194320 | tf_op jit(solution)/shard_map/all_gather | solution.py:101
  184.1 3.0 convolution_convert_fusion
  187.1 0.8 fusion.30
  187.9 4.4 %multiply_reduce_fusion.1 = (f32[512,2]{0,1:T(2,128)S(1)}, f32[512,512]{0,1:T(8,128)S(1)}) fusion(f32[512,512]{0,1:T(8,128)S(1)} %fusion.30, bf16[512,3840]{0,1:T(8,128)(2,1)} %bitcast.1, bf16[3840,512]{1,0:T(8,128)(2,1)S(1)} %copy-done.8), kind=kOutput, calls=%fused_computation.44 | convolution fusion | flops 2014051328 | bytes 9965568 | tf_op jit(solution)/shard_map/dot_general | solution.py:87
  192.7 0.9 fusion.35
  194.2 3.1 fusion.5
  197.3 4.4 %fusion = (f32[2,512]{1,0:T(2,128)S(1)}, f32[1536,512,2]{1,0,2:T(8,128)S(1)}) fusion(f32[2,512]{1,0:T(2,128)S(1)} %get-tuple-element.20, f32[1536,512,2]{1,0,2:T(8,128)S(1)} %get-tuple-element.21, pred[512,1536]{0,1:T(8,128)(4,1)S(1)} %copy-done.3, bf16[64,2,8,256]{3,2,1,0:T(8,128)(2,1)S(1)} %bitcast.142, bf16[512,1,256]{2,0,1:T(8,128)(2,1)} %fusion.34, ...), kind=kOutput, calls=%fused_computation.3 | convolution fusion | flops 815528960 | bytes 14688256 | tf_op jit(solution)/shard_map/tngd,knd->ngtk/dot_general | solution.py:56
  201.7 3.8 %fusion.26 = f32[512,2,256]{2,0,1:T(8,128)S(1)} fusion(f32[1536,512,2]{1,0,2:T(8,128)S(1)} %get-tuple-element.23, f32[2,512]{1,0:T(2,128)S(1)} %get-tuple-element.22, f32[2,512]{1,0:T(2,128)S(1)} %get-tuple-element.20, f32[1536,512,2]{1,0,2:T(8,128)S(1)} %get-tuple-element.21, pred[512,1536]{0,1:T(8,128)(4,1)S(1)} %copy-done.3, ...), kind=kOutput, calls=%fused_computation.31 | convolution fusion | flops 819462144 | bytes 15212544 | tf_op jit(solution)/shard_map/ngtk,knd->tngd/dot_general | solution.py:59
  207.3 4.5 %fusion.74 = f32[64,64,512]{2,1,0:T(8,128)} fusion(bf16[64,16,64]{2,1,0:T(8,128)(2,1)S(1)} %bitcast.133, bf16[64,16,512]{2,1,0:T(8,128)(2,1)S(1)} %bitcast.132), kind=kOutput, calls=%fused_computation.107 | convolution fusion | flops 67108864 | bytes 9568256 | tf_op jit(solution)/shard_map/acr,ace->are/dot_general | solution.py:170
  211.8 5.2 %fusion.31 = bf16[256,2,512]{2,0,1:T(8,128)(2,1)S(1)} fusion(f32[2,512]{1,0:T(2,128)S(1)} %get-tuple-element.20, f32[1536,512,2]{1,0,2:T(8,128)} %copy-done.11, pred[512,1536]{0,1:T(8,128)(4,1)S(1)} %copy-done.3, bf16[512,1,256]{2,0,1:T(8,128)(2,1)} %fusion.34, bf16[512,1,256]{2,0,1:T(8,128)(2,1)} %collective-permute-done.1, ...), kind=kOutput, calls=%fused_computation.35 | convolution fusion | flops 814219264 | bytes 8392704 | tf_op jit(solution)/shard_map/ngtk,knd->tngd/dot_general | solution.py:55
  217.0 1.0 copy.53
  218.0 143.3 %reduce-scatter.2.cloned.1.call-done = f32[1,64,512]{2,1,0:T(8,128)} async-done(((f32[64,64,512]{2,1,0:T(8,128)}), f32[1,64,512]{2,1,0:T(8,128)}) %reduce-scatter.2.cloned.1.call-update) | async-done | bytes 131088 | tf_op jit(solution)/shard_map/reduce_scatter | solution.py:169
  (63 shorter events, 5.4 us)
Async XLA Ops:
  7.2 55.1 %copy-start = (bf16[3840,256]{1,0:T(8,128)(2,1)S(1)}, bf16[3840,256]{1,0:T(8,128)(2,1)}, u32[]{:S(2)}) copy-start(bf16[3840,256]{1,0:T(8,128)(2,1)} %param.13) | copy-start | bytes 5898244
  7.2 98.3 %all-gather.3.cloned.1.call-start = ((), (), s32[]{:S(2)}) async-start(), calls=%async_computation.2 | async-start | bytes 8519680 | tf_op jit(solution)/shard_map/all_gather | solution.py:100
  7.9 176.2 %all-gather.5.cloned.1.call-start = ((), (), s32[]{:S(2)}) async-start(), calls=%async_computation.3 | async-start | bytes 4259840 | tf_op jit(solution)/shard_map/all_gather | solution.py:101
  12.1 7.2 %copy-start.6 = (s32[512]{0:T(512)S(1)}, s32[512]{0:T(512)}, u32[]{:S(2)}) copy-start(s32[512]{0:T(512)} %param.20) | copy-start | bytes 6148
  12.1 11.2 %copy-start.4 = (s32[512,1]{0,1:T(1,128)S(1)}, s32[512,1]{0,1:T(1,128)}, u32[]{:S(2)}) copy-start(s32[512,1]{0,1:T(1,128)} %param.19) | copy-start | bytes 6148
  12.1 13.9 %copy-start.2 = (bf16[512,960]{0,1:T(8,128)(2,1)S(1)}, bf16[512,960]{0,1:T(8,128)(2,1)}, u32[]{:S(2)}) copy-start(bf16[512,960]{0,1:T(8,128)(2,1)} %param.11) | copy-start | bytes 2949124
  12.1 50.2 %all-to-all-start = ((bf16[4,512,960]{1,2,0:T(8,128)(2,1)}), bf16[4,512,960]{1,2,0:T(8,128)(2,1)}, u32[]{:S(2)}, u32[]{:S(2)}) async-start(bf16[4,512,960]{1,2,0:T(8,128)(2,1)} %stack.2), calls=%async_computation | async-start | bytes 7864320 | tf_op jit(solution)/shard_map/all_to_all | solution.py:85
  19.2 342.1 %reduce-scatter.2.cloned.1.call-start = ((), (), s32[]{:S(2)}) async-start(), calls=%async_computation.4 | async-start | bytes 8519680 | tf_op jit(solution)/shard_map/reduce_scatter | solution.py:169
  19.2 13.2 %collective-permute-start.3 = (s32[512]{0:T(512)S(1)}, s32[512]{0:T(512)S(1)}, u32[]{:S(2)}, u32[]{:S(2)}) collective-permute-start(s32[512]{0:T(512)S(1)} %copy-done.6), channel_id=1, source_target_pairs={{0,4},{4,8},{8,12},{12,16},{16,20},{20,24},{24,28},{28,32},{32,36}... | collective-permute-start | bytes 6152 | tf_op jit(solution)/shard_map/ppermute | solution.py:18
  20.5 11.9 %collective-permute-start.2 = (s32[512]{0:T(512)S(1)}, s32[512]{0:T(512)S(1)}, u32[]{:S(2)}, u32[]{:S(2)}) collective-permute-start(s32[512]{0:T(512)S(1)} %copy-done.6), channel_id=1, source_target_pairs={{0,8},{4,12},{8,16},{12,20},{16,24},{20,28},{24,32},{28,36},{32,40... | collective-permute-start | bytes 6152 | tf_op jit(solution)/shard_map/ppermute | solution.py:18
  62.2 4.0 %copy-start.7 = (f32[256]{0:T(256)S(1)}, f32[256]{0:T(256)}, u32[]{:S(2)}) copy-start(f32[256]{0:T(256)} %param.16) | copy-start | bytes 3076
  62.2 12.4 %copy-start.9 = (bf16[3840,256]{1,0:T(8,128)(2,1)S(1)}, bf16[3840,256]{1,0:T(8,128)(2,1)}, u32[]{:S(2)}) copy-start(bf16[3840,256]{1,0:T(8,128)(2,1)} %param.14) | copy-start | bytes 5898244
  68.3 125.8 %collective-permute-start.5 = (bf16[512,1,256]{0,2,1:T(8,128)(2,1)}, bf16[512,1,256]{0,2,1:T(8,128)(2,1)}, u32[]{:S(2)}, u32[]{:S(2)}) collective-permute-start(bf16[512,1,256]{0,2,1:T(8,128)(2,1)} %pad_maximum_fusion), channel_id=1, source_target_pairs={{0,4},{4,8},{8,12},{12,16},{16,20},{20,24},{24,28},{28,32},{32,36}... | collective-permute-start | bytes 786440 | tf_op jit(solution)/shard_map/ppermute | solution.py:18
  70.3 123.9 %collective-permute-start.4 = (bf16[512,1,256]{0,2,1:T(8,128)(2,1)}, bf16[512,1,256]{0,2,1:T(8,128)(2,1)}, u32[]{:S(2)}, u32[]{:S(2)}) collective-permute-start(bf16[512,1,256]{0,2,1:T(8,128)(2,1)} %pad_maximum_fusion), channel_id=1, source_target_pairs={{0,8},{4,12},{8,16},{12,20},{16,24},{20,28},{24,32},{28,36},{32,40... | collective-permute-start | bytes 786440 | tf_op jit(solution)/shard_map/ppermute | solution.py:18
  78.7 118.5 %collective-permute-start.1 = (bf16[512,1,256]{2,0,1:T(8,128)(2,1)}, bf16[512,1,256]{2,0,1:T(8,128)(2,1)}, u32[]{:S(2)}, u32[]{:S(2)}) collective-permute-start(bf16[512,1,256]{2,0,1:T(8,128)(2,1)} %fusion.34), channel_id=1, source_target_pairs={{0,4},{4,8},{8,12},{12,16},{16,20},{20,24},{24,28},{28,32},{32,36}... | collective-permute-start | bytes 786440 | tf_op jit(solution)/shard_map/ppermute | solution.py:18
  82.8 114.4 %collective-permute-start = (bf16[512,1,256]{2,0,1:T(8,128)(2,1)}, bf16[512,1,256]{2,0,1:T(8,128)(2,1)}, u32[]{:S(2)}, u32[]{:S(2)}) collective-permute-start(bf16[512,1,256]{2,0,1:T(8,128)(2,1)} %fusion.34), channel_id=1, source_target_pairs={{0,8},{4,12},{8,16},{12,20},{16,24},{20,28},{24,32},{28,36},{32,40... | collective-permute-start | bytes 786440 | tf_op jit(solution)/shard_map/ppermute | solution.py:18
  184.1 3.8 %copy-start.8 = (bf16[3840,512]{1,0:T(8,128)(2,1)S(1)}, bf16[3840,512]{1,0:T(8,128)(2,1)}, u32[]{:S(2)}) copy-start(bf16[3840,512]{1,0:T(8,128)(2,1)} %param.12) | copy-start | bytes 11796484
  192.3 1.4 copy-start.5
  192.7 1.5 copy-start.3
  194.2 3.1 copy-start.10
  197.3 4.5 %copy-start.11 = (f32[1536,512,2]{1,0,2:T(8,128)}, f32[1536,512,2]{1,0,2:T(8,128)S(1)}, u32[]{:S(2)}) copy-start(f32[1536,512,2]{1,0,2:T(8,128)S(1)} %get-tuple-element.21) | copy-start | bytes 18874372
  211.8 149.6 %copy-start.1 = (bf16[3840,256]{1,0:T(8,128)(2,1)S(1)}, bf16[3840,256]{1,0:T(8,128)(2,1)}, u32[]{:S(2)}) copy-start(bf16[3840,256]{1,0:T(8,128)(2,1)} %param.13) | copy-start | bytes 5898244
Sparse Core Ops, SparseCore 0:
  10.8 94.6 all-gather.2
  108.2 75.8 all-gather.4
  211.9 149.3 reduce-scatter.1
